TPU v7x, 32 devices: a whole 2x2x4 slice. The times are simulated.
32 devices in a mesh: cplx: 4 (over y, core), dap: 8 (over z, x).
Axes of the slice: x: 2, y: 2, z: 4, core: 2. Of those that a mesh axis runs over, the one named last changes fastest.
Arguments:
- alignment_features: bfloat16 [64, 64, 256], P(('cplx', 'dap')), parts along dimension 0, may hold values from -6 to 6
- couple_features: bfloat16 [256, 64, 128], P(('cplx', 'dap')), parts along dimension 0, may hold values from -6 to 6
- alignment_presence: int32 [64, 64], P('cplx'), parts along dimension 0, may hold values 0 or 1
- amino_presence: int32 [256], P('cplx'), parts along dimension 0, may hold values 0 or 1
- strand_identity: int32 [256], P('cplx'), parts along dimension 0, may hold values from 0 to 3, never falling along the last dimension, each value on 1 to 32 neighbouring positions
- strand_couple_embedding: float32 [2, 128], replicated, may hold values from -4 to 4
- fourfold_input_matrix: bfloat16 [256, 1024], replicated, may hold values from -0.375 to 0.375
- heads_merge_matrix: bfloat16 [256, 256], replicated, may hold values from -1.5 to 1.5
- couple_logit_matrix: bfloat16 [128, 8], replicated, may hold values from -30 to 30
- twin_factor_matrix: bfloat16 [256, 64], replicated, may hold values from -0.375 to 0.375
- tensor_reduce_matrix: bfloat16 [1024, 128], replicated, may hold values from -0.75 to 0.75
Outputs:
- alignment_mixed: bfloat16 [64, 64, 256], P(('cplx', 'dap')), parts along dimension 0
- couple_refreshed: bfloat16 [256, 64, 128], P(('cplx', 'dap')), parts along dimension 0
There are 4 independent parts, one for each index of `cplx`. A program takes and returns all parts, laid end to end along the dimension named above; an argument that names none is the same for every part. Nothing has to cross between parts.
All inputs are finite; a program needn't handle non-finite values.
Results may differ from a plain program's by a relative error of at most 0.0075.
The roundings to bfloat16 on the way count: a program that leaves them out, or rounds other values in their place, can miss the bound.
Values may be sent and summed in bfloat16 or wider, within the bound.
No kernel may reach another device: no remote copies, remote signals or barrier semaphores. Data moves between devices by JAX's collectives and lax.ppermute only.
A program may use at most 64 MiB of HBM per device.

v0:
```python
import jax
import jax.numpy as jnp
from jax import lax
from jax.sharding import PartitionSpec as P

EPS = 1e-05


def standardize_features(x):
    x = x.astype(jnp.float32)
    center = x - jnp.mean(x, axis=-1, keepdims=True)
    spread = jnp.mean(center * center, axis=-1, keepdims=True)
    return center * lax.rsqrt(spread + EPS)


def on_device(
    alignment_features,
    couple_features,
    alignment_presence,
    amino_presence,
    strand_identity,
    strand_couple_embedding,
    fourfold_input_matrix,
    heads_merge_matrix,
    couple_logit_matrix,
    twin_factor_matrix,
    tensor_reduce_matrix,
):
    res_here = couple_features.shape[0]
    every_amino_line = couple_features.shape[1]
    device_aligned_lines = alignment_features.shape[0]
    width = twin_factor_matrix.shape[1] // 2
    head_count = couple_logit_matrix.shape[1]
    head_size = heads_merge_matrix.shape[0] // head_count
    position = lax.axis_index("dap")
    res_start = position * res_here
    seq_start = position * device_aligned_lines
    chain_here = lax.dynamic_slice_in_dim(strand_identity, res_start, res_here)
    same = (chain_here[:, None] == strand_identity[None, :]).astype(jnp.float32)[..., None]
    z_in = (
        couple_features.astype(jnp.float32)
        + (1.0 - same) * strand_couple_embedding[0]
        + same * strand_couple_embedding[1]
    )
    pair_ln = standardize_features(z_in).astype(jnp.bfloat16)
    bias_here = jnp.einsum(
        "ijc,ch->hij", pair_ln, couple_logit_matrix, preferred_element_type=jnp.float32
    ).astype(jnp.bfloat16)
    bias_all = lax.all_gather(bias_here, "dap", axis=1, tiled=True)
    presence_numeric = alignment_presence.astype(jnp.float32)
    mask_rows = lax.dynamic_slice_in_dim(presence_numeric, seq_start, device_aligned_lines, 0)
    standardized_alignment = standardize_features(alignment_features).astype(jnp.bfloat16)
    mapped_lines = jnp.dot(
        standardized_alignment.reshape(
            device_aligned_lines * every_amino_line, alignment_features.shape[2]
        ),
        fourfold_input_matrix,
        preferred_element_type=jnp.float32,
    )
    mapped_lines = mapped_lines.reshape(
        device_aligned_lines, every_amino_line, 4, head_count, head_size
    )
    asking_vectors = (mapped_lines[:, :, 0] * head_size ** (-0.5)).astype(jnp.bfloat16)
    target_vectors = mapped_lines[:, :, 1].astype(jnp.bfloat16)
    content_vectors = mapped_lines[:, :, 2].astype(jnp.bfloat16)
    sigmoid_factors = jax.nn.sigmoid(mapped_lines[:, :, 3])
    scores = jnp.einsum(
        "sihd,sjhd->shij", asking_vectors, target_vectors, preferred_element_type=jnp.float32
    )
    scores = (
        scores
        + bias_all.astype(jnp.float32)[None]
        + ((mask_rows - 1.0) * 1000000000.0)[:, None, None, :]
    )
    weights = jax.nn.softmax(scores, axis=-1).astype(jnp.bfloat16)
    context = jnp.einsum(
        "shij,sjhd->sihd", weights, content_vectors, preferred_element_type=jnp.float32
    )
    gated_values = (
        (sigmoid_factors * context)
        .astype(jnp.bfloat16)
        .reshape(device_aligned_lines * every_amino_line, head_count * head_size)
    )
    offset_lines = jnp.dot(
        gated_values, heads_merge_matrix, preferred_element_type=jnp.float32
    ).reshape(alignment_features.shape)
    alignment_mixed = (alignment_features.astype(jnp.float32) + offset_lines).astype(jnp.bfloat16)
    mask_cols = lax.dynamic_slice_in_dim(presence_numeric, res_start, res_here, 1)
    count = jnp.dot(mask_cols.T, presence_numeric, precision=lax.Precision.HIGHEST) + 1.0
    rows_ln = standardize_features(alignment_mixed).astype(jnp.bfloat16)
    twin_factor_features = jnp.einsum(
        "sjm,mk->jsk", rows_ln, twin_factor_matrix, preferred_element_type=jnp.float32
    )
    mask_t = mask_rows.T[..., None]
    left_rows = (
        (twin_factor_features[:, :, :width] * mask_t)
        .astype(jnp.bfloat16)
        .reshape(every_amino_line, device_aligned_lines * width)
    )
    right_rows = (
        (twin_factor_features[:, :, width:] * mask_t)
        .astype(jnp.bfloat16)
        .reshape(every_amino_line, device_aligned_lines * width)
    )
    left_full = lax.all_to_all(left_rows, "dap", split_axis=0, concat_axis=1, tiled=True)
    piece = lax.all_gather(right_rows, "dap", axis=1, tiled=True)
    columns = piece.shape[1]
    left_part = left_full.reshape(res_here, columns // width, width)
    right_part = piece.reshape(every_amino_line, columns // width, width)
    outer = jnp.einsum("isc,jse->ijce", left_part, right_part, preferred_element_type=jnp.float32)
    outer = outer.astype(jnp.bfloat16).reshape(res_here, every_amino_line, width * width)
    update = (
        jnp.einsum("ijk,kz->ijz", outer, tensor_reduce_matrix, preferred_element_type=jnp.float32)
        / count[..., None]
    )
    resf = amino_presence.astype(jnp.float32)
    res_local = lax.dynamic_slice_in_dim(resf, res_start, res_here)
    pair_mask = res_local[:, None] * resf[None, :]
    couple_refreshed = (z_in + pair_mask[..., None] * update).astype(jnp.bfloat16)
    return (alignment_mixed, couple_refreshed)


def solution(mesh):
    in_specs = (
        P(("cplx", "dap"), None, None),
        P(("cplx", "dap"), None, None),
        P("cplx", None),
        P("cplx"),
        P("cplx"),
        P(),
        P(),
        P(),
        P(),
        P(),
        P(),
    )
    out_specs = (P(("cplx", "dap"), None, None), P(("cplx", "dap"), None, None))
    return jax.shard_map(
        on_device, mesh=mesh, in_specs=in_specs, out_specs=out_specs, check_vma=False
    )
```

profile of v0, /device:TPU:0, one launch (start us, length us, event | category | flops | bytes accessed | tf_op | source)
XLA Modules:
  0.0 88.1 jit_solution(13455693065240458379)
XLA Ops:
  0.6 0.0 copy-start
  0.6 0.0 copy-start.1
  0.7 0.8 dynamic_slice.12
  1.4 0.7 broadcast_subtract_fusion
  2.2 0.7 compare_convert_fusion
  2.9 0.9 %convert_reduce_fusion = f32[2,64]{1,0:T(2,128)S(1)} fusion(bf16[2,64,256]{2,1,0:T(8,128)(2,1)} %param.11), kind=kLoop, calls=%fused_computation.35 | loop fusion | flops 65408 | bytes 66048 | tf_op jit(solution)/shard_map/reduce_sum | solution.py:11
  3.8 1.0 %fusion.24 = f32[2,64]{1,0:T(2,128)S(1)} fusion(bf16[2,64,256]{2,1,0:T(8,128)(2,1)} %param.11, f32[2,64]{1,0:T(2,128)S(1)} %broadcast_multiply_fusion.3), kind=kLoop, calls=%fused_computation.42 | loop fusion | flops 130944 | bytes 66560 | tf_op jit(solution)/shard_map/reduce_sum | solution.py:12
  4.9 0.8 slice_bitcast_fusion.5
  5.6 1.2 %fusion.19 = f32[8,64]{1,0:T(8,128)S(1)} fusion(bf16[8,64,128]{2,1,0:T(8,128)(2,1)} %param.12, f32[128]{0:T(128)S(1)} %get-tuple-element.7, f32[8,64]{1,0:T(8,128)S(1)} %compare_convert_fusion, f32[128]{0:T(128)S(1)} %get-tuple-element.6, f32[8,64]{1,0:T(8,128)S(1)} %broadcast_subtract_fusion), kind=kLoop, calls=%fused_computation.33 | loop fusion | flops 392704 | bytes 138240 | tf_op jit(solution)/shard_map/reduce_sum | solution.py:11
  6.9 1.3 %multiply_reduce_fusion = f32[8,64]{1,0:T(8,128)S(1)} fusion(bf16[8,64,128]{2,1,0:T(8,128)(2,1)} %param.12, f32[8,64]{1,0:T(8,128)S(1)} %broadcast_multiply_fusion.1, f32[128]{0:T(128)S(1)} %get-tuple-element.7, f32[8,64]{1,0:T(8,128)S(1)} %compare_convert_fusion, f32[128]{0:T(128)S(1)} %get-tuple-element.6, f32[8,64]{1,0:T(8,128)S(1)} %broadcast_subtract_fusion), kind=kLoop, calls=%fused_computation.30 | loop fusion | flops 523776 | bytes 140288 | tf_op jit(solution)/shard_map/reduce_sum | solution.py:12
  8.2 0.7 convert_element_type.94
  8.9 1.4 %fusion.10 = bf16[8,8,64]{2,0,1:T(8,128)(2,1)S(1)} fusion(bf16[8,64,128]{2,1,0:T(8,128)(2,1)} %param.12, f32[8,64]{1,0:T(8,128)S(1)} %add_rsqrt_fusion, f32[8,64]{1,0:T(8,128)S(1)} %broadcast_multiply_fusion.1, f32[128]{0:T(128)S(1)} %get-tuple-element.7, f32[8,64]{1,0:T(8,128)S(1)} %compare_convert_fusion, f32[128]{0:T(128)S(1)} %get-tuple-element.6, ...), kind=kOutput, calls=%fused_computation.17 | convolution fusion | flops 1576960 | bytes 150528 | tf_op jit(solution)/shard_map/ijc,ch->hij/dot_general | solution.py:46
  10.2 32.3 %all_gather.6 = bf16[8,64,64]{2,0,1:T(8,128)(2,1)S(1)} all-gather(bf16[8,8,64]{2,0,1:T(8,128)(2,1)S(1)} %fusion.10), channel_id=1, replica_groups=mesh['cplx'=4,'dap'=8] {'dap'}, dimensions={1}, use_global_device_ids=true | all-gather | bytes 73728 | tf_op jit(solution)/shard_map/all_gather | solution.py:49
  42.6 0.1 copy.28
  42.7 1.2 %copy.27 = bf16[256,1024]{0,1:T(8,128)(2,1)S(1)} copy(bf16[256,1024]{1,0:T(8,128)(2,1)} %param.17) | data formatting | bytes 1048576 | tf_op args[6]
  44.0 0.0 copy-done.1
  44.0 0.4 fusion.49
  44.4 0.3 fusion.3
  44.7 0.0 copy-start.4
  44.7 0.1 fusion.50
  44.8 0.0 copy-start.5
  44.8 0.0 copy-start.6
  44.9 0.2 fusion.7
  45.1 0.5 copy-done.4
  45.6 0.3 convert_reduce_fusion.1
  45.9 0.0 copy-start.3
  45.9 0.2 fusion.26
  46.1 0.0 copy-done.5
  46.1 0.2 convolution_bitcast_fusion.1
  46.3 0.1 copy.31
  46.4 0.1 all_to_all.12
  46.5 0.7 reshape.178
  47.2 5.5 %all-to-all-start = ((bf16[8,2,256]{2,1,0:T(2,128)(2,1)}), bf16[8,2,256]{2,1,0:T(2,128)(2,1)S(1)}, u32[]{:S(2)}, u32[]{:S(2)}) async-start(bf16[8,2,256]{2,1,0:T(2,128)(2,1)} %reshape.178), calls=%async_computation | async-start | bytes 16384 | tf_op jit(solution)/shard_map/all_to_all | solution.py:105
  52.7 0.3 convolution_add_fusion.2
  53.0 0.0 copy-done.6
  53.0 0.1 dynamic_slice.14
  53.1 0.1 broadcast_multiply_fusion
  53.1 31.1 %all_gather.7 = bf16[64,512]{0,1:T(8,128)(2,1)S(1)} all-gather(bf16[64,64]{0,1:T(8,128)(2,1)S(1)} %bitcast.75), channel_id=1, replica_groups=mesh['cplx'=4,'dap'=8] {'dap'}, dimensions={1}, use_global_device_ids=true | all-gather | bytes 73728 | tf_op jit(solution)/shard_map/all_gather | solution.py:106
  84.2 0.0 all-to-all-done
  84.2 0.1 reshape.179
  84.3 0.1 reshape.175
  84.4 0.7 convert_bitcast_fusion
  85.1 0.0 copy-start.2
  85.1 1.4 %copy.34 = bf16[8,64,32,32]{1,3,2,0:T(8,128)(2,1)S(1)} copy(bf16[8,64,32,32]{1,2,0,3:T(8,128)(2,1)S(1)} %convert_bitcast_fusion) | data formatting | bytes 2097152 | tf_op jit(solution)/shard_map/convert_element_type | solution.py:111
  86.5 0.0 copy-done.3
  86.5 0.0 copy-done
  86.5 0.0 copy-done.2
  86.5 1.6 %fusion.8 = bf16[8,64,128]{2,1,0:T(8,128)(2,1)} fusion(bf16[8,64,1024]{1,2,0:T(8,128)(2,1)S(1)} %bitcast.72, bf16[1024,128]{1,0:T(8,128)(2,1)S(1)} %copy-done, bf16[8,64,128]{2,1,0:T(8,128)(2,1)S(1)} %copy-done.2, f32[8,64]{1,0:T(8,128)S(1)} %convolution_add_fusion.2, f32[8,64]{1,0:T(8,128)S(1)} %broadcast_multiply_fusion, f32[128]{0:T(128)S(1)} %get-tuple-element.7, ...), kind=kOutput, calls=%fused_computation.12 | convolution fusion | flops 134807552 | bytes 1582080 | tf_op jit(solution)/shard_map/ijk,kz->ijz/dot_general | solution.py:113
  (10 shorter events, 0.1 us)
Async XLA Ops:
  0.6 85.9 %copy-start = (bf16[1024,128]{1,0:T(8,128)(2,1)S(1)}, bf16[1024,128]{1,0:T(8,128)(2,1)}, u32[]{:S(2)}) copy-start(bf16[1024,128]{1,0:T(8,128)(2,1)} %param.21) | copy-start | bytes 786436
  0.6 43.3 %copy-start.1 = (bf16[2,64,256]{2,1,0:T(8,128)(2,1)S(1)}, bf16[2,64,256]{2,1,0:T(8,128)(2,1)}, u32[]{:S(2)}) copy-start(bf16[2,64,256]{2,1,0:T(8,128)(2,1)} %param.11) | copy-start | bytes 196612
  44.7 0.9 %copy-start.4 = (bf16[256,256]{1,0:T(8,128)(2,1)S(1)}, bf16[256,256]{1,0:T(8,128)(2,1)}, u32[]{:S(2)}) copy-start(bf16[256,256]{1,0:T(8,128)(2,1)} %param.18) | copy-start | bytes 393220
  44.8 1.2 %copy-start.5 = (bf16[256,64]{0,1:T(8,128)(2,1)S(1)}, bf16[256,64]{0,1:T(8,128)(2,1)}, u32[]{:S(2)}) copy-start(bf16[256,64]{0,1:T(8,128)(2,1)} %param.20) | copy-start | bytes 98308
  44.8 8.1 %copy-start.6 = (s32[64]{0:T(128)S(1)}, s32[64]{0:T(128)}, u32[]{:S(2)}) copy-start(s32[64]{0:T(128)} %param.14) | copy-start | bytes 772
  45.9 40.6 %copy-start.3 = (bf16[2,64,256]{2,1,0:T(8,128)(2,1)}, bf16[2,64,256]{2,1,0:T(8,128)(2,1)S(1)}, u32[]{:S(2)}) copy-start(bf16[2,64,256]{2,1,0:T(8,128)(2,1)S(1)} %get-tuple-element.11) | copy-start | bytes 196612
  47.2 37.0 %all-to-all-start = ((bf16[8,2,256]{2,1,0:T(2,128)(2,1)}), bf16[8,2,256]{2,1,0:T(2,128)(2,1)S(1)}, u32[]{:S(2)}, u32[]{:S(2)}) async-start(bf16[8,2,256]{2,1,0:T(2,128)(2,1)} %reshape.178), calls=%async_computation | async-start | bytes 16384 | tf_op jit(solution)/shard_map/all_to_all | solution.py:105
  85.1 1.4 %copy-start.2 = (bf16[8,64,128]{2,1,0:T(8,128)(2,1)S(1)}, bf16[8,64,128]{2,1,0:T(8,128)(2,1)}, u32[]{:S(2)}) copy-start(bf16[8,64,128]{2,1,0:T(8,128)(2,1)} %param.12) | copy-start | bytes 393220
where the time goes:
time: 88.6 us; the launch traced here: 88.1 us
  blocking collectives  63.4 us (72%)
  other arithmetic  7.06 us (8%)
  local copies, waits for them, and re-layouts  5.95 us (7%)
  starting transfers between devices  5.47 us (6%)
  matrix products  5.34 us (6%)
    all_gather x1, blocking collectives, on_device(): bias_all = lax.all_gather(bias_here, 'dap', axis=1, tiled=True)  32.3 us
    all_gather x1, blocking collectives, on_device(): piece = lax.all_gather(right_rows, 'dap', axis=1, tiled=True)  31.1 us
    all_to_all x1, starting transfers between devices, on_device(): lax.all_to_all(left_rows, 'dap', split_axis=0, concat_axis=1, tiled=True)  5.47 us
    unnamed x17, local copies, waits for them, and re-layouts  2.54 us
    reduce_sum x3, other arithmetic, standardize_features(): spread = jnp.mean(center * center, axis=-1, keepdims=True)  2.46 us
    reduce_sum x2, other arithmetic, standardize_features(): center = x - jnp.mean(x, axis=-1, keepdims=True)  2.16 us
  transfers between devices with their start and end apart: 1, of which 0 were waited for; matrix products, arithmetic and copies ran while one was open for 0% of the time, Pallas kernels for 0%

commit v1 on v0

--- a/solution.py
+++ b/solution.py
@@ -46,7 +46,11 @@
     bias_here = jnp.einsum(
         "ijc,ch->hij", pair_ln, couple_logit_matrix, preferred_element_type=jnp.float32
     ).astype(jnp.bfloat16)
-    bias_all = lax.all_gather(bias_here, "dap", axis=1, tiled=True)
+    length = lax.axis_size("dap")
+    repeats = [length if d == 1 else 1 for d in range(bias_here.ndim)]
+    bias_all = lax.all_to_all(
+        jnp.tile(bias_here, repeats), "dap", split_axis=1, concat_axis=1, tiled=True
+    )
     presence_numeric = alignment_presence.astype(jnp.float32)
     mask_rows = lax.dynamic_slice_in_dim(presence_numeric, seq_start, device_aligned_lines, 0)
     standardized_alignment = standardize_features(alignment_features).astype(jnp.bfloat16)

time: 88.6 us -> 65.3 us (0.74)
  blocking collectives: 63.4 us -> 31 us
  starting transfers between devices: 5.47 us -> 10.6 us
  waiting for transfers between devices: 0.01 us -> 3.33 us
    all_gather x1 -> x0, blocking collectives: 32.3 us -> none  [on_device(): bias_all = lax.all_gather(bias_here, 'dap', axis=1, tiled=True)]
    all_to_all x0 -> x1, starting transfers between devices: none -> 7.28 us  [on_device(): lax.all_to_all(jnp.tile(bias_here, repeats), 'dap', split_axis=1, concat_...]
    all_to_all x0 -> x1, waiting for transfers between devices: none -> 3.33 us  [on_device(): lax.all_to_all(jnp.tile(bias_here, repeats), 'dap', split_axis=1, concat_...]
    all_to_all x1, starting transfers between devices: 5.47 us -> 3.33 us  [on_device(): lax.all_to_all(left_rows, 'dap', split_axis=0, concat_axis=1, tiled=True)]
    unnamed x17 -> x19, local copies, waits for them, and re-layouts: 2.54 us -> 2.44 us
  transfers between devices with their start and end apart: 1 -> 2, of which waited for: 0 -> 1; matrix products, arithmetic and copies ran while one was open for 0% -> 5% of each run, Pallas kernels for 0% -> 0%
where the time goes in v1:
time: 65.3 us; the launch traced here: 64.8 us
  blocking collectives  31 us (47%)
  starting transfers between devices  10.6 us (16%)
  other arithmetic  7.72 us (12%)
  local copies, waits for them, and re-layouts  5.89 us (9%)
  matrix products  5.34 us (8%)
  waiting for transfers between devices  3.33 us (5%)
  between operations  0.91 us (1%)
    all_gather x1, blocking collectives, on_device(): piece = lax.all_gather(right_rows, 'dap', axis=1, tiled=True)  31 us
    all_to_all x1, starting transfers between devices, on_device(): lax.all_to_all(jnp.tile(bias_here, repeats), 'dap', split_axis=1, concat_...  7.28 us
    all_to_all x1, starting transfers between devices, on_device(): lax.all_to_all(left_rows, 'dap', split_axis=0, concat_axis=1, tiled=True)  3.33 us
    all_to_all x1, waiting for transfers between devices, on_device(): lax.all_to_all(jnp.tile(bias_here, repeats), 'dap', split_axis=1, concat_...  3.33 us
    reduce_sum x3, other arithmetic, standardize_features(): spread = jnp.mean(center * center, axis=-1, keepdims=True)  2.46 us
    unnamed x19, local copies, waits for them, and re-layouts  2.44 us
    reduce_sum x2, other arithmetic, standardize_features(): center = x - jnp.mean(x, axis=-1, keepdims=True)  2.16 us
    dot_general x1, matrix products, on_device(): jnp.einsum('ijk,kz->ijz', outer, tensor_reduce_matrix, preferred_element_...  1.55 us
  transfers between devices with their start and end apart: 2, of which 1 were waited for; matrix products, arithmetic and copies ran while one was open for 5% of the time, Pallas kernels for 0%

profile of v1, /device:TPU:0, one launch (start us, length us, event | category | flops | bytes accessed | tf_op | source)
XLA Modules:
  0.0 64.8 jit_solution(12735926835115421875)
XLA Ops:
  0.6 0.0 copy-start
  0.6 0.0 copy-start.1
  0.7 0.0 copy-start.2
  0.7 0.7 %convert_element_type.98 = f32[64]{0:T(128)S(1)} convert(s32[64]{0:T(128)} %param.14) | non-fusion elementwise | flops 64 | bytes 512 | tf_op jit(solution)/shard_map/convert_element_type | solution.py:120
  1.4 0.7 %dynamic_slice.12 = s32[8]{0:T(128)S(1)} dynamic-slice(s32[64]{0:T(128)} %param.15, s32[]{:T(128)S(6)} %select_n.8), dynamic_slice_sizes={8} | dynamic-slice | bytes 68 | tf_op jit(solution)/shard_map/dynamic_slice | solution.py:38
  2.1 0.1 dynamic_slice.14
  2.2 0.8 %slice_bitcast_fusion.5 = (f32[128]{0:T(128)S(1)}, f32[128]{0:T(128)S(1)}) fusion(f32[2,128]{1,0:T(2,128)} %param.16), kind=kLoop, calls=%fused_computation.77 | loop fusion | bytes 2048 | tf_op jit(solution)/shard_map/mul | solution.py:42
  3.0 0.7 %compare_convert_fusion = f32[8,64]{1,0:T(8,128)S(1)} fusion(s32[64]{0:T(128)} %param.15, s32[8]{0:T(128)S(1)} %dynamic_slice.12), kind=kLoop, calls=%fused_computation.66 | loop fusion | flops 1024 | bytes 2336 | tf_op jit(solution)/shard_map/convert_element_type | solution.py:39
  3.7 0.7 %broadcast_multiply_fusion = (f32[8,64]{1,0:T(8,128)S(1)}, f32[8,64]{1,0:T(8,128)S(1)}) fusion(f32[64]{0:T(128)S(1)} %convert_element_type.98, f32[8]{0:T(128)S(1)} %dynamic_slice.14, s32[64]{0:T(128)} %param.15, s32[8]{0:T(128)S(1)} %dynamic_slice.12), kind=kLoop, calls=%fused_computation.68 | loop fusion | flops 2048 | bytes 4672 | tf_op jit(solution)/shard_map/mul | solution.py:122
  4.4 1.2 %fusion.19 = f32[8,64]{1,0:T(8,128)S(1)} fusion(bf16[8,64,128]{2,1,0:T(8,128)(2,1)} %param.12, f32[128]{0:T(128)S(1)} %get-tuple-element.7, f32[8,64]{1,0:T(8,128)S(1)} %compare_convert_fusion, f32[128]{0:T(128)S(1)} %get-tuple-element.6, f32[8,64]{1,0:T(8,128)S(1)} %get-tuple-element.13), kind=kLoop, calls=%fused_computation.33 | loop fusion | flops 392704 | bytes 138240 | tf_op jit(solution)/shard_map/reduce_sum | solution.py:11
  5.7 1.3 %multiply_reduce_fusion = f32[8,64]{1,0:T(8,128)S(1)} fusion(bf16[8,64,128]{2,1,0:T(8,128)(2,1)} %param.12, f32[8,64]{1,0:T(8,128)S(1)} %broadcast_multiply_fusion.1, f32[128]{0:T(128)S(1)} %get-tuple-element.7, f32[8,64]{1,0:T(8,128)S(1)} %compare_convert_fusion, f32[128]{0:T(128)S(1)} %get-tuple-element.6, f32[8,64]{1,0:T(8,128)S(1)} %get-tuple-element.13), kind=kLoop, calls=%fused_computation.30 | loop fusion | flops 523776 | bytes 140288 | tf_op jit(solution)/shard_map/reduce_sum | solution.py:12
  7.0 1.4 %fusion.10 = bf16[8,8,64]{2,0,1:T(8,128)(2,1)S(1)} fusion(bf16[8,64,128]{2,1,0:T(8,128)(2,1)} %param.12, f32[8,64]{1,0:T(8,128)S(1)} %add_rsqrt_fusion, f32[8,64]{1,0:T(8,128)S(1)} %broadcast_multiply_fusion.1, f32[128]{0:T(128)S(1)} %get-tuple-element.7, f32[8,64]{1,0:T(8,128)S(1)} %compare_convert_fusion, f32[128]{0:T(128)S(1)} %get-tuple-element.6, ...), kind=kOutput, calls=%fused_computation.17 | convolution fusion | flops 1576960 | bytes 150528 | tf_op jit(solution)/shard_map/ijc,ch->hij/dot_general | solution.py:46
  8.4 0.1 copy.49
  8.5 0.8 %reshape.182 = bf16[8,2,2048]{2,1,0:T(2,128)(2,1)} reshape(bf16[64,8,64]{2,1,0:T(8,128)(2,1)S(1)} %bitcast.81) | data formatting | bytes 131072
  9.3 7.3 %all-to-all-start = ((bf16[8,2,2048]{2,1,0:T(2,128)(2,1)}), bf16[8,2,2048]{2,1,0:T(2,128)(2,1)S(1)}, u32[]{:S(2)}, u32[]{:S(2)}) async-start(bf16[8,2,2048]{2,1,0:T(2,128)(2,1)} %reshape.182), calls=%async_computation | async-start | bytes 131072 | tf_op jit(solution)/shard_map/all_to_all | solution.py:51
  16.5 0.9 %convert_reduce_fusion = f32[2,64]{1,0:T(2,128)S(1)} fusion(bf16[2,64,256]{2,1,0:T(8,128)(2,1)} %param.11), kind=kLoop, calls=%fused_computation.35 | loop fusion | flops 65408 | bytes 66048 | tf_op jit(solution)/shard_map/reduce_sum | solution.py:11
  17.5 1.0 %fusion.24 = f32[2,64]{1,0:T(2,128)S(1)} fusion(bf16[2,64,256]{2,1,0:T(8,128)(2,1)} %param.11, f32[2,64]{1,0:T(2,128)S(1)} %broadcast_multiply_fusion.3), kind=kLoop, calls=%fused_computation.42 | loop fusion | flops 130944 | bytes 66560 | tf_op jit(solution)/shard_map/reduce_sum | solution.py:12
  18.5 0.7 %convert_element_type.94 = f32[16,64]{1,0:T(8,128)S(1)} convert(s32[16,64]{1,0:T(8,128)} %param.13) | non-fusion elementwise | flops 1024 | bytes 8192 | tf_op jit(solution)/shard_map/convert_element_type | solution.py:54
  19.2 0.0 copy-done.2
  19.2 0.2 copy.28
  19.4 0.0 copy-done.1
  19.4 0.4 fusion.49
  19.8 0.3 convolution_add_fusion.2
  20.1 3.3 %all-to-all-done = bf16[8,2,2048]{2,1,0:T(2,128)(2,1)S(1)} async-done(((bf16[8,2,2048]{2,1,0:T(2,128)(2,1)}), bf16[8,2,2048]{2,1,0:T(2,128)(2,1)S(1)}, u32[]{:S(2)}, u32[]{:S(2)}) %all-to-all-start) | async-done | bytes 65568 | tf_op jit(solution)/shard_map/all_to_all | solution.py:51
  23.4 0.1 reshape.183
  23.6 0.1 copy.31
  23.7 0.3 fusion.3
  24.0 0.0 copy-start.5
  24.0 0.1 fusion.50
  24.2 0.0 copy-start.6
  24.2 0.2 fusion.7
  24.4 0.5 copy-done.5
  24.9 0.3 convert_reduce_fusion.1
  25.2 0.0 copy-start.4
  25.2 0.2 fusion.26
  25.4 0.0 copy-done.6
  25.4 0.2 convolution_bitcast_fusion.1
  25.7 0.1 copy.34
  25.8 0.1 all_to_all.16
  25.9 0.7 %reshape.184 = bf16[8,2,256]{2,1,0:T(2,128)(2,1)} reshape(bf16[8,8,64]{2,1,0:T(8,128)(2,1)S(1)} %all_to_all.16) | data formatting | bytes 16384
  26.6 3.3 %all-to-all-start.1 = ((bf16[8,2,256]{2,1,0:T(2,128)(2,1)}), bf16[8,2,256]{2,1,0:T(2,128)(2,1)S(1)}, u32[]{:S(2)}, u32[]{:S(2)}) async-start(bf16[8,2,256]{2,1,0:T(2,128)(2,1)} %reshape.184), calls=%async_computation.1 | async-start | bytes 16384 | tf_op jit(solution)/shard_map/all_to_all | solution.py:109
  29.9 31.0 %all_gather.3 = bf16[64,512]{0,1:T(8,128)(2,1)S(1)} all-gather(bf16[64,64]{0,1:T(8,128)(2,1)S(1)} %bitcast.83), channel_id=1, replica_groups=mesh['cplx'=4,'dap'=8] {'dap'}, dimensions={1}, use_global_device_ids=true | all-gather | bytes 73728 | tf_op jit(solution)/shard_map/all_gather | solution.py:110
  60.9 0.0 all-to-all-done.1
  60.9 0.1 reshape.185
  61.0 0.1 reshape.179
  61.1 0.7 %convert_bitcast_fusion = bf16[8,64,32,32]{1,2,0,3:T(8,128)(2,1)S(1)} fusion(bf16[8,16,32,1]{2,1,0,3:T(8,128)(2,1)S(1)} %reshape.179, bf16[64,16,32,1]{0,2,1,3:T(8,128)(2,1)S(1)} %bitcast.79), kind=kOutput, calls=%fused_computation.1 | convolution fusion | flops 17301504 | bytes 1122304 | tf_op jit(solution)/shard_map/isc,jse->ijce/dot_general | solution.py:114
  61.8 0.0 copy-start.3
  61.9 1.4 %copy.37 = bf16[8,64,32,32]{1,3,2,0:T(8,128)(2,1)S(1)} copy(bf16[8,64,32,32]{1,2,0,3:T(8,128)(2,1)S(1)} %convert_bitcast_fusion) | data formatting | bytes 2097152 | tf_op jit(solution)/shard_map/convert_element_type | solution.py:115
  63.2 0.0 copy-done.4
  63.2 0.0 copy-done
  63.2 0.0 copy-done.3
  63.3 1.6 %fusion.8 = bf16[8,64,128]{2,1,0:T(8,128)(2,1)} fusion(bf16[8,64,1024]{1,2,0:T(8,128)(2,1)S(1)} %bitcast.78, bf16[1024,128]{1,0:T(8,128)(2,1)S(1)} %copy-done, bf16[8,64,128]{2,1,0:T(8,128)(2,1)S(1)} %copy-done.3, f32[8,64]{1,0:T(8,128)S(1)} %convolution_add_fusion.2, f32[8,64]{1,0:T(8,128)S(1)} %get-tuple-element.12, f32[128]{0:T(128)S(1)} %get-tuple-element.7, ...), kind=kOutput, calls=%fused_computation.12 | convolution fusion | flops 134807552 | bytes 1582080 | tf_op jit(solution)/shard_map/ijk,kz->ijz/dot_general | solution.py:117
  (11 shorter events, 0.1 us)
Async XLA Ops:
  0.6 62.6 %copy-start = (bf16[1024,128]{1,0:T(8,128)(2,1)S(1)}, bf16[1024,128]{1,0:T(8,128)(2,1)}, u32[]{:S(2)}) copy-start(bf16[1024,128]{1,0:T(8,128)(2,1)} %param.21) | copy-start | bytes 786436
  0.6 18.8 %copy-start.1 = (bf16[2,64,256]{2,1,0:T(8,128)(2,1)S(1)}, bf16[2,64,256]{2,1,0:T(8,128)(2,1)}, u32[]{:S(2)}) copy-start(bf16[2,64,256]{2,1,0:T(8,128)(2,1)} %param.11) | copy-start | bytes 196612
  0.7 18.6 %copy-start.2 = (bf16[256,1024]{1,0:T(8,128)(2,1)S(1)}, bf16[256,1024]{1,0:T(8,128)(2,1)}, u32[]{:S(2)}) copy-start(bf16[256,1024]{1,0:T(8,128)(2,1)} %param.17) | copy-start | bytes 1572868
  9.3 14.2 %all-to-all-start = ((bf16[8,2,2048]{2,1,0:T(2,128)(2,1)}), bf16[8,2,2048]{2,1,0:T(2,128)(2,1)S(1)}, u32[]{:S(2)}, u32[]{:S(2)}) async-start(bf16[8,2,2048]{2,1,0:T(2,128)(2,1)} %reshape.182), calls=%async_computation | async-start | bytes 131072 | tf_op jit(solution)/shard_map/all_to_all | solution.py:51
  24.0 0.9 %copy-start.5 = (bf16[256,256]{1,0:T(8,128)(2,1)S(1)}, bf16[256,256]{1,0:T(8,128)(2,1)}, u32[]{:S(2)}) copy-start(bf16[256,256]{1,0:T(8,128)(2,1)} %param.18) | copy-start | bytes 393220
  24.2 1.2 %copy-start.6 = (bf16[256,64]{0,1:T(8,128)(2,1)S(1)}, bf16[256,64]{0,1:T(8,128)(2,1)}, u32[]{:S(2)}) copy-start(bf16[256,64]{0,1:T(8,128)(2,1)} %param.20) | copy-start | bytes 98308
  25.2 38.0 %copy-start.4 = (bf16[2,64,256]{2,1,0:T(8,128)(2,1)}, bf16[2,64,256]{2,1,0:T(8,128)(2,1)S(1)}, u32[]{:S(2)}) copy-start(bf16[2,64,256]{2,1,0:T(8,128)(2,1)S(1)} %get-tuple-element.11) | copy-start | bytes 196612
  26.6 34.3 %all-to-all-start.1 = ((bf16[8,2,256]{2,1,0:T(2,128)(2,1)}), bf16[8,2,256]{2,1,0:T(2,128)(2,1)S(1)}, u32[]{:S(2)}, u32[]{:S(2)}) async-start(bf16[8,2,256]{2,1,0:T(2,128)(2,1)} %reshape.184), calls=%async_computation.1 | async-start | bytes 16384 | tf_op jit(solution)/shard_map/all_to_all | solution.py:109
  61.8 1.4 %copy-start.3 = (bf16[8,64,128]{2,1,0:T(8,128)(2,1)S(1)}, bf16[8,64,128]{2,1,0:T(8,128)(2,1)}, u32[]{:S(2)}) copy-start(bf16[8,64,128]{2,1,0:T(8,128)(2,1)} %param.12) | copy-start | bytes 393220
